TPU v7x, 512 devices: a whole 4x4x16 slice. The times are simulated.
512 devices in a mesh: segment: 2 (over x_lo), seq: 32 (over z, core), tensor: 8 (over y, x_hi).
Axes of the slice: x: 4 (x_hi: 2, x_lo: 2; x = x_hi * 2 + x_lo), y: 4, z: 16, core: 2. Of those that a mesh axis runs over, the one named last changes fastest.
Arguments:
- vision_states: bfloat16 [6144, 7680], P(('segment', 'seq'), 'tensor'), may hold values from -6 to 6
- kv_weight: bfloat16 [7680, 2048], P('tensor'), may hold values from -0.09375 to 0.09375
- key_gain: float32 [128], replicated, may hold values from 0.5 to 1.5
- queries: bfloat16 [16384, 8, 1024], P('seq', 'tensor', 'segment'), may hold values from -700 to 700
- tile_tokens: int32 [4], replicated, may hold values from 768 to 1536, as said below
- text_tiles: int32 [16384, 2], P('seq'), may hold values from 0 to 4, as said below
Outputs:
- attended: bfloat16 [16384, 8, 1024], P('seq', 'tensor', 'segment')
Inputs may be any that keep to these rules, and one draw needn't show every extreme that they name: The valid tokens of tile i are its first tile_tokens[i] positions of 1536; some tile is full. Text token r sees tiles text_tiles[r, 0] to text_tiles[r, 1] - 1, with text_tiles[r, 0] <= text_tiles[r, 1]; an empty range means it sees no image.
All inputs are finite; a program needn't handle non-finite values.
Results may differ from a plain program's by a relative error of at most 0.012.
The roundings to bfloat16 on the way count: a program that leaves them out, or rounds other values in their place, can miss the bound.
Values may be sent and summed in bfloat16 or wider, within the bound.
A program may use at most 64 MiB of HBM per device.

v0:
```python
import jax
import jax.numpy as jnp
from jax import lax
from jax.sharding import PartitionSpec as P


def block_count(total_rows, limit_rows):
    for parts_count in range(1, total_rows + 1):
        if total_rows % parts_count == 0 and total_rows // parts_count <= limit_rows:
            return parts_count
    return total_rows


def visibility(positions, tile_len, tile_tokens, lower, upper):
    tile_ids = positions // tile_len
    within_tile = positions % tile_len
    tile_table = jnp.arange(tile_tokens.shape[0], dtype=jnp.int32)
    valid_count = jnp.sum(
        jnp.where(tile_ids[:, None] == tile_table[None, :], tile_tokens[None, :], 0), axis=-1
    )
    key_valid = within_tile < valid_count
    return (
        key_valid[None, :]
        & (tile_ids[None, :] >= lower[:, None])
        & (tile_ids[None, :] < upper[:, None])
    )


def update(running, query_heads, kv_piece, visible, score_scale, head_dim):
    row_max, row_sum, summed = running
    scores = (
        jnp.einsum(
            "rkhd,knd->rkhn",
            query_heads,
            kv_piece[:, :, :head_dim],
            preferred_element_type=jnp.float32,
        )
        * score_scale
    )
    key_mask = visible[:, None, None, :]
    masked = jnp.where(key_mask, scores, -1e30)
    new_max = jnp.maximum(row_max, jnp.max(masked, axis=-1))
    factor = jnp.exp(row_max - new_max)
    expterm = jnp.where(key_mask, jnp.exp(masked - new_max[..., None]), 0.0)
    row_sum = row_sum * factor + jnp.sum(expterm, axis=-1)
    weights = expterm.astype(jnp.bfloat16)
    summed = summed * factor[..., None] + jnp.einsum(
        "rkhn,knd->rkhd", weights, kv_piece[:, :, head_dim:], preferred_element_type=jnp.float32
    )
    return (new_max, row_sum, summed)


def shards(vision_states, kv_weight, key_gain, queries, tile_tokens, text_tiles):
    head_dim = key_gain.shape[0]
    key_rows = vision_states.shape[0]
    all_heads = kv_weight.shape[1] // (2 * head_dim)
    local_heads = all_heads // lax.axis_size("tensor")
    weight_heads = kv_weight.reshape(kv_weight.shape[0], all_heads, 2 * head_dim)
    sums = lax.psum_scatter(
        jnp.einsum("rd,dch->crh", vision_states, weight_heads, preferred_element_type=jnp.float32),
        "tensor",
        scatter_dimension=0,
        tiled=True,
    )
    keys_raw = sums[:, :, :head_dim]
    mean_sq = jnp.mean(keys_raw * keys_raw, axis=-1, keepdims=True)
    normed = keys_raw * lax.rsqrt(mean_sq + 1e-05) * key_gain
    kv_block = jnp.concatenate([normed, sums[:, :, head_dim:]], axis=-1).astype(jnp.bfloat16)
    segment_count = lax.axis_size("segment")
    seq_count = lax.axis_size("seq")
    tile_len = key_rows * segment_count * seq_count // tile_tokens.shape[0]
    text_rows = queries.shape[0]
    query_count = queries.shape[2] // head_dim
    query_heads = queries.reshape(text_rows, local_heads, query_count, head_dim)
    lower = text_tiles[:, 0]
    upper = text_tiles[:, 1]
    unseen = (upper <= lower).astype(jnp.float32)
    score_scale = head_dim ** (-0.5)
    start_state = (
        jnp.full((text_rows, local_heads, query_count), -1e30, jnp.float32),
        jnp.zeros((text_rows, local_heads, query_count), jnp.float32),
        jnp.zeros((text_rows, local_heads, query_count, head_dim), jnp.float32),
    )
    gathered = lax.all_gather(kv_block, ("segment", "seq"), axis=1, tiled=True)
    total_rows = gathered.shape[1]
    blocks = block_count(total_rows, 768)
    block_rows = total_rows // blocks

    def one_block(block_index, state_now):
        block_piece = lax.dynamic_slice_in_dim(gathered, block_index * block_rows, block_rows, 1)
        local_rows = block_index * block_rows + jnp.arange(block_rows, dtype=jnp.int32)
        visible = visibility(local_rows, tile_len, tile_tokens, lower, upper)
        return update(state_now, query_heads, block_piece, visible, score_scale, head_dim)

    row_max, row_sum, summed = lax.fori_loop(0, blocks, one_block, start_state)
    attended = summed / (row_sum + unseen[:, None, None])[..., None]
    return attended.reshape(text_rows, local_heads, query_count * head_dim).astype(jnp.bfloat16)


def solution(mesh):
    placed = (
        P(("segment", "seq"), "tensor"),
        P("tensor", None),
        P(),
        P("seq", "tensor", "segment"),
        P(),
        P("seq", None),
    )
    return jax.shard_map(
        shards, mesh=mesh, in_specs=placed, out_specs=P("seq", "tensor", "segment"), check_vma=False
    )
```

profile of v0, /device:TPU:1, one launch (start us, length us, event | category | flops | bytes accessed | tf_op | source)
XLA Modules:
  0.0 335.9 jit_solution(15315524799468415300)
XLA Ops:
  6.6 0.9 copy-done
  7.5 3.8 %fusion.30 = f32[8,96,256]{2,1,0:T(8,128)} fusion(bf16[120,8,8,256]{3,2,1,0:T(8,128)(2,1)} %bitcast.107, bf16[96,960]{1,0:T(8,128)(2,1)S(1)} %copy-done), kind=kOutput, calls=%fused_computation.41 | convolution fusion | flops 377487360 | bytes 4902912 | tf_op jit(solution)/shard_map/rd,dch->crh/dot_general | solution.py:60
  11.3 90.3 %reduce-scatter.2.cloned.1.call-done = f32[1,96,256]{2,1,0:T(8,128)} async-done(((f32[8,96,256]{2,1,0:T(8,128)}), f32[1,96,256]{2,1,0:T(8,128)}) %reduce-scatter.2.cloned.1.call-update) | async-done | bytes 98320 | tf_op jit(solution)/shard_map/reduce_scatter | solution.py:59
  101.6 0.9 multiply_reduce_fusion
  102.5 0.8 slice.46
  103.3 0.9 multiply_convert_fusion
  104.2 0.6 pad_maximum_fusion
  104.9 0.2 copy.20
  105.1 0.3 copy.21
  105.5 124.5 %all-gather.2.cloned.1.call-done = bf16[1,6144,256]{2,1,0:T(8,128)(2,1)} async-done(((bf16[1,96,256]{2,1,0:T(8,128)(2,1)}), bf16[1,6144,256]{2,1,0:T(8,128)(2,1)}) %all-gather.2.cloned.1.call-update) | async-done | bytes 3145744 | tf_op jit(solution)/shard_map/all_gather | solution.py:84
  229.9 98.0 %while.20 = (s32[]{:T(128)}, f32[512,1,4]{0,2,1:T(4,128)S(1)}, f32[512,1,4]{0,2,1:T(4,128)S(1)}, f32[512,1,4,128]{0,3,2,1:T(8,128)S(1)}, s32[4]{0:T(128)S(1)}, /...) while((s32[]{:T(128)}, f32[512,1,4]{0,2,1:T(4,128)S(1)}, ...), condition=%wide.region_6.7_spmd.clone, body=%wide.region_2.6_spmd.clone.sunk | while | flops 828146688 | bytes 48780040 | solution.py:95
  229.9 0.1 select_reduce_fusion.2
  230.1 0.5 compare_and_fusion.2
  230.5 4.8 %fusion.43 = (f32[512,4]{0,1:T(4,128)S(1)}, f32[768,512,4]{1,0,2:T(8,128)}) fusion(pred[512,768]{0,1:T(8,128)(4,1)S(1)} %compare_and_fusion.2, bf16[512,1,4,128]{3,0,2,1:T(8,128)(2,1)S(1)} %get-tuple-element.402, bf16[1,6144,256]{2,1,0:T(8,128)(2,1)} %get-tuple-element.401, s32[]{:T(128)S(6)} %select_n.147), kind=kOutput, calls=%fused_computation.2.clone.1 | convolution fusion | flops 407369728 | bytes 7413764 | tf_op jit(solution)/shard_map/while/body/eval_jaxpr/rkhd,knd->rkhn/dot_general | solution.py:32
  235.4 5.2 %fusion.46 = f32[512,1,4,128]{0,3,2,1:T(8,128)S(1)} fusion(f32[768,512,4]{1,0,2:T(8,128)} %get-tuple-element.364, f32[512,4]{0,1:T(4,128)S(1)} %bitcast.100, pred[512,768]{0,1:T(8,128)(4,1)S(1)} %compare_and_fusion.2, f32[512,1,4,128]{0,3,2,1:T(8,128)S(1)} %get-tuple-element.383, f32[512,4]{0,1:T(4,128)S(1)} %get-tuple-element.365, ...), kind=kOutput, calls=%fused_computation.10.clone.1 | convolution fusion | flops 411303936 | bytes 8994825 | tf_op jit(solution)/shard_map/while/body/eval_jaxpr/rkhn,knd->rkhd/dot_general | solution.py:47
  240.6 1.6 fusion.45
  242.2 0.1 select_reduce_fusion.2
  242.3 0.5 compare_and_fusion.2
  242.8 4.8 %fusion.43 = (f32[512,4]{0,1:T(4,128)S(1)}, f32[768,512,4]{1,0,2:T(8,128)}) fusion(pred[512,768]{0,1:T(8,128)(4,1)S(1)} %compare_and_fusion.2, bf16[512,1,4,128]{3,0,2,1:T(8,128)(2,1)S(1)} %get-tuple-element.402, bf16[1,6144,256]{2,1,0:T(8,128)(2,1)} %get-tuple-element.401, s32[]{:T(128)S(6)} %select_n.147), kind=kOutput, calls=%fused_computation.2.clone.1 | convolution fusion | flops 407369728 | bytes 7413764 | tf_op jit(solution)/shard_map/while/body/eval_jaxpr/rkhd,knd->rkhn/dot_general | solution.py:32
  247.6 5.2 %fusion.46 = f32[512,1,4,128]{0,3,2,1:T(8,128)S(1)} fusion(f32[768,512,4]{1,0,2:T(8,128)} %get-tuple-element.364, f32[512,4]{0,1:T(4,128)S(1)} %bitcast.100, pred[512,768]{0,1:T(8,128)(4,1)S(1)} %compare_and_fusion.2, f32[512,1,4,128]{0,3,2,1:T(8,128)S(1)} %get-tuple-element.383, f32[512,4]{0,1:T(4,128)S(1)} %get-tuple-element.365, ...), kind=kOutput, calls=%fused_computation.10.clone.1 | convolution fusion | flops 411303936 | bytes 8994825 | tf_op jit(solution)/shard_map/while/body/eval_jaxpr/rkhn,knd->rkhd/dot_general | solution.py:47
  252.8 1.6 fusion.45
  254.5 0.1 select_reduce_fusion.2
  254.6 0.5 compare_and_fusion.2
  255.1 4.8 %fusion.43 = (f32[512,4]{0,1:T(4,128)S(1)}, f32[768,512,4]{1,0,2:T(8,128)}) fusion(pred[512,768]{0,1:T(8,128)(4,1)S(1)} %compare_and_fusion.2, bf16[512,1,4,128]{3,0,2,1:T(8,128)(2,1)S(1)} %get-tuple-element.402, bf16[1,6144,256]{2,1,0:T(8,128)(2,1)} %get-tuple-element.401, s32[]{:T(128)S(6)} %select_n.147), kind=kOutput, calls=%fused_computation.2.clone.1 | convolution fusion | flops 407369728 | bytes 7413764 | tf_op jit(solution)/shard_map/while/body/eval_jaxpr/rkhd,knd->rkhn/dot_general | solution.py:32
  259.9 5.2 %fusion.46 = f32[512,1,4,128]{0,3,2,1:T(8,128)S(1)} fusion(f32[768,512,4]{1,0,2:T(8,128)} %get-tuple-element.364, f32[512,4]{0,1:T(4,128)S(1)} %bitcast.100, pred[512,768]{0,1:T(8,128)(4,1)S(1)} %compare_and_fusion.2, f32[512,1,4,128]{0,3,2,1:T(8,128)S(1)} %get-tuple-element.383, f32[512,4]{0,1:T(4,128)S(1)} %get-tuple-element.365, ...), kind=kOutput, calls=%fused_computation.10.clone.1 | convolution fusion | flops 411303936 | bytes 8994825 | tf_op jit(solution)/shard_map/while/body/eval_jaxpr/rkhn,knd->rkhd/dot_general | solution.py:47
  265.1 1.6 fusion.45
  266.8 0.5 compare_and_fusion.2
  267.3 4.8 %fusion.43 = (f32[512,4]{0,1:T(4,128)S(1)}, f32[768,512,4]{1,0,2:T(8,128)}) fusion(pred[512,768]{0,1:T(8,128)(4,1)S(1)} %compare_and_fusion.2, bf16[512,1,4,128]{3,0,2,1:T(8,128)(2,1)S(1)} %get-tuple-element.402, bf16[1,6144,256]{2,1,0:T(8,128)(2,1)} %get-tuple-element.401, s32[]{:T(128)S(6)} %select_n.147), kind=kOutput, calls=%fused_computation.2.clone.1 | convolution fusion | flops 407369728 | bytes 7413764 | tf_op jit(solution)/shard_map/while/body/eval_jaxpr/rkhd,knd->rkhn/dot_general | solution.py:32
  272.1 5.2 %fusion.46 = f32[512,1,4,128]{0,3,2,1:T(8,128)S(1)} fusion(f32[768,512,4]{1,0,2:T(8,128)} %get-tuple-element.364, f32[512,4]{0,1:T(4,128)S(1)} %bitcast.100, pred[512,768]{0,1:T(8,128)(4,1)S(1)} %compare_and_fusion.2, f32[512,1,4,128]{0,3,2,1:T(8,128)S(1)} %get-tuple-element.383, f32[512,4]{0,1:T(4,128)S(1)} %get-tuple-element.365, ...), kind=kOutput, calls=%fused_computation.10.clone.1 | convolution fusion | flops 411303936 | bytes 8994825 | tf_op jit(solution)/shard_map/while/body/eval_jaxpr/rkhn,knd->rkhd/dot_general | solution.py:47
  277.3 1.6 fusion.45
  279.1 0.5 compare_and_fusion.2
  279.6 4.8 %fusion.43 = (f32[512,4]{0,1:T(4,128)S(1)}, f32[768,512,4]{1,0,2:T(8,128)}) fusion(pred[512,768]{0,1:T(8,128)(4,1)S(1)} %compare_and_fusion.2, bf16[512,1,4,128]{3,0,2,1:T(8,128)(2,1)S(1)} %get-tuple-element.402, bf16[1,6144,256]{2,1,0:T(8,128)(2,1)} %get-tuple-element.401, s32[]{:T(128)S(6)} %select_n.147), kind=kOutput, calls=%fused_computation.2.clone.1 | convolution fusion | flops 407369728 | bytes 7413764 | tf_op jit(solution)/shard_map/while/body/eval_jaxpr/rkhd,knd->rkhn/dot_general | solution.py:32
  284.4 5.2 %fusion.46 = f32[512,1,4,128]{0,3,2,1:T(8,128)S(1)} fusion(f32[768,512,4]{1,0,2:T(8,128)} %get-tuple-element.364, f32[512,4]{0,1:T(4,128)S(1)} %bitcast.100, pred[512,768]{0,1:T(8,128)(4,1)S(1)} %compare_and_fusion.2, f32[512,1,4,128]{0,3,2,1:T(8,128)S(1)} %get-tuple-element.383, f32[512,4]{0,1:T(4,128)S(1)} %get-tuple-element.365, ...), kind=kOutput, calls=%fused_computation.10.clone.1 | convolution fusion | flops 411303936 | bytes 8994825 | tf_op jit(solution)/shard_map/while/body/eval_jaxpr/rkhn,knd->rkhd/dot_general | solution.py:47
  289.6 1.6 fusion.45
  291.3 0.5 compare_and_fusion.2
  291.8 4.8 %fusion.43 = (f32[512,4]{0,1:T(4,128)S(1)}, f32[768,512,4]{1,0,2:T(8,128)}) fusion(pred[512,768]{0,1:T(8,128)(4,1)S(1)} %compare_and_fusion.2, bf16[512,1,4,128]{3,0,2,1:T(8,128)(2,1)S(1)} %get-tuple-element.402, bf16[1,6144,256]{2,1,0:T(8,128)(2,1)} %get-tuple-element.401, s32[]{:T(128)S(6)} %select_n.147), kind=kOutput, calls=%fused_computation.2.clone.1 | convolution fusion | flops 407369728 | bytes 7413764 | tf_op jit(solution)/shard_map/while/body/eval_jaxpr/rkhd,knd->rkhn/dot_general | solution.py:32
  296.6 5.2 %fusion.46 = f32[512,1,4,128]{0,3,2,1:T(8,128)S(1)} fusion(f32[768,512,4]{1,0,2:T(8,128)} %get-tuple-element.364, f32[512,4]{0,1:T(4,128)S(1)} %bitcast.100, pred[512,768]{0,1:T(8,128)(4,1)S(1)} %compare_and_fusion.2, f32[512,1,4,128]{0,3,2,1:T(8,128)S(1)} %get-tuple-element.383, f32[512,4]{0,1:T(4,128)S(1)} %get-tuple-element.365, ...), kind=kOutput, calls=%fused_computation.10.clone.1 | convolution fusion | flops 411303936 | bytes 8994825 | tf_op jit(solution)/shard_map/while/body/eval_jaxpr/rkhn,knd->rkhd/dot_general | solution.py:47
  301.8 1.6 fusion.45
  303.6 0.5 compare_and_fusion.2
  304.1 4.8 %fusion.43 = (f32[512,4]{0,1:T(4,128)S(1)}, f32[768,512,4]{1,0,2:T(8,128)}) fusion(pred[512,768]{0,1:T(8,128)(4,1)S(1)} %compare_and_fusion.2, bf16[512,1,4,128]{3,0,2,1:T(8,128)(2,1)S(1)} %get-tuple-element.402, bf16[1,6144,256]{2,1,0:T(8,128)(2,1)} %get-tuple-element.401, s32[]{:T(128)S(6)} %select_n.147), kind=kOutput, calls=%fused_computation.2.clone.1 | convolution fusion | flops 407369728 | bytes 7413764 | tf_op jit(solution)/shard_map/while/body/eval_jaxpr/rkhd,knd->rkhn/dot_general | solution.py:32
  308.9 5.2 %fusion.46 = f32[512,1,4,128]{0,3,2,1:T(8,128)S(1)} fusion(f32[768,512,4]{1,0,2:T(8,128)} %get-tuple-element.364, f32[512,4]{0,1:T(4,128)S(1)} %bitcast.100, pred[512,768]{0,1:T(8,128)(4,1)S(1)} %compare_and_fusion.2, f32[512,1,4,128]{0,3,2,1:T(8,128)S(1)} %get-tuple-element.383, f32[512,4]{0,1:T(4,128)S(1)} %get-tuple-element.365, ...), kind=kOutput, calls=%fused_computation.10.clone.1 | convolution fusion | flops 411303936 | bytes 8994825 | tf_op jit(solution)/shard_map/while/body/eval_jaxpr/rkhn,knd->rkhd/dot_general | solution.py:47
  314.1 1.6 fusion.45
  315.8 0.5 compare_and_fusion.2
  316.3 4.8 %fusion.43 = (f32[512,4]{0,1:T(4,128)S(1)}, f32[768,512,4]{1,0,2:T(8,128)}) fusion(pred[512,768]{0,1:T(8,128)(4,1)S(1)} %compare_and_fusion.2, bf16[512,1,4,128]{3,0,2,1:T(8,128)(2,1)S(1)} %get-tuple-element.402, bf16[1,6144,256]{2,1,0:T(8,128)(2,1)} %get-tuple-element.401, s32[]{:T(128)S(6)} %select_n.147), kind=kOutput, calls=%fused_computation.2.clone.1 | convolution fusion | flops 407369728 | bytes 7413764 | tf_op jit(solution)/shard_map/while/body/eval_jaxpr/rkhd,knd->rkhn/dot_general | solution.py:32
  321.1 5.2 %fusion.46 = f32[512,1,4,128]{0,3,2,1:T(8,128)S(1)} fusion(f32[768,512,4]{1,0,2:T(8,128)} %get-tuple-element.364, f32[512,4]{0,1:T(4,128)S(1)} %bitcast.100, pred[512,768]{0,1:T(8,128)(4,1)S(1)} %compare_and_fusion.2, f32[512,1,4,128]{0,3,2,1:T(8,128)S(1)} %get-tuple-element.383, f32[512,4]{0,1:T(4,128)S(1)} %get-tuple-element.365, ...), kind=kOutput, calls=%fused_computation.10.clone.1 | convolution fusion | flops 411303936 | bytes 8994825 | tf_op jit(solution)/shard_map/while/body/eval_jaxpr/rkhn,knd->rkhd/dot_general | solution.py:47
  326.3 1.6 fusion.45
  328.0 0.1 divide_convert_fusion
  328.1 1.0 copy.25
  (79 shorter events, 1.1 us)
Async XLA Ops:
  6.5 0.9 copy-start
  6.5 98.4 %copy-start.2 = (bf16[512,1,512]{2,0,1:T(8,128)(2,1)S(1)}, bf16[512,1,512]{2,0,1:T(8,128)(2,1)}, u32[]{:S(2)}) copy-start(bf16[512,1,512]{2,0,1:T(8,128)(2,1)} %param.11) | copy-start | bytes 1572868
  6.5 98.9 %copy-start.3 = (s32[512,2]{0,1:T(2,128)S(1)}, s32[512,2]{0,1:T(2,128)}, u32[]{:S(2)}) copy-start(s32[512,2]{0,1:T(2,128)} %param.13) | copy-start | bytes 12292
  6.5 223.4 %copy-start.4 = (s32[4]{0:T(128)S(1)}, s32[4]{0:T(128)}, u32[]{:S(2)}) copy-start(s32[4]{0:T(128)} %param.12) | copy-start | bytes 52
  6.5 95.0 %reduce-scatter.2.cloned.1.call-start = ((), (), s32[]{:S(2)}) async-start(), calls=%async_computation.1 | async-start | bytes 884736 | tf_op jit(solution)/shard_map/reduce_scatter | solution.py:59
  11.2 218.7 %all-gather.2.cloned.1.call-start = ((), (), s32[]{:S(2)}) async-start(), calls=%async_computation.2 | async-start | bytes 3194880 | tf_op jit(solution)/shard_map/all_gather | solution.py:84
  235.4 5.2 %copy-start.1 = (f32[768,512,4]{1,0,2:T(8,128)S(1)}, f32[768,512,4]{1,0,2:T(8,128)}, u32[]{:S(2)}) copy-start(f32[768,512,4]{1,0,2:T(8,128)} %get-tuple-element.364) | copy-start | bytes 18874372 | tf_op jit(solution)/shard_map/while
  247.6 5.2 %copy-start.1 = (f32[768,512,4]{1,0,2:T(8,128)S(1)}, f32[768,512,4]{1,0,2:T(8,128)}, u32[]{:S(2)}) copy-start(f32[768,512,4]{1,0,2:T(8,128)} %get-tuple-element.364) | copy-start | bytes 18874372 | tf_op jit(solution)/shard_map/while
  259.9 5.2 %copy-start.1 = (f32[768,512,4]{1,0,2:T(8,128)S(1)}, f32[768,512,4]{1,0,2:T(8,128)}, u32[]{:S(2)}) copy-start(f32[768,512,4]{1,0,2:T(8,128)} %get-tuple-element.364) | copy-start | bytes 18874372 | tf_op jit(solution)/shard_map/while
  272.1 5.2 %copy-start.1 = (f32[768,512,4]{1,0,2:T(8,128)S(1)}, f32[768,512,4]{1,0,2:T(8,128)}, u32[]{:S(2)}) copy-start(f32[768,512,4]{1,0,2:T(8,128)} %get-tuple-element.364) | copy-start | bytes 18874372 | tf_op jit(solution)/shard_map/while
  284.4 5.2 %copy-start.1 = (f32[768,512,4]{1,0,2:T(8,128)S(1)}, f32[768,512,4]{1,0,2:T(8,128)}, u32[]{:S(2)}) copy-start(f32[768,512,4]{1,0,2:T(8,128)} %get-tuple-element.364) | copy-start | bytes 18874372 | tf_op jit(solution)/shard_map/while
  296.6 5.2 %copy-start.1 = (f32[768,512,4]{1,0,2:T(8,128)S(1)}, f32[768,512,4]{1,0,2:T(8,128)}, u32[]{:S(2)}) copy-start(f32[768,512,4]{1,0,2:T(8,128)} %get-tuple-element.364) | copy-start | bytes 18874372 | tf_op jit(solution)/shard_map/while
  308.9 5.2 %copy-start.1 = (f32[768,512,4]{1,0,2:T(8,128)S(1)}, f32[768,512,4]{1,0,2:T(8,128)}, u32[]{:S(2)}) copy-start(f32[768,512,4]{1,0,2:T(8,128)} %get-tuple-element.364) | copy-start | bytes 18874372 | tf_op jit(solution)/shard_map/while
  321.1 5.2 %copy-start.1 = (f32[768,512,4]{1,0,2:T(8,128)S(1)}, f32[768,512,4]{1,0,2:T(8,128)}, u32[]{:S(2)}) copy-start(f32[768,512,4]{1,0,2:T(8,128)} %get-tuple-element.364) | copy-start | bytes 18874372 | tf_op jit(solution)/shard_map/while
Sparse Core Ops, SparseCore 0:
  11.8 89.7 reduce-scatter.1
  105.0 124.9 all-gather.1
where the time goes:
time: 336 us
  waiting for transfers between devices  215 us (64%)
  matrix products  83.5 us (25%)
  other arithmetic  20.1 us (6%)
  between operations  13.5 us (4%)
    all_gather x1, waiting for transfers between devices, shards(): gathered = lax.all_gather(kv_block, ('segment', 'seq'), axis=1, tiled=True)  124 us
    reduce_scatter x1, waiting for transfers between devices, shards(): lax.psum_scatter(jnp.einsum('rd,dch->crh', vision_states, weight_heads, p...  90.3 us
    dot_general x8, matrix products, update(): jnp.einsum('rkhn,knd->rkhd', weights, kv_piece[:, :, head_dim:], preferre...  41.4 us
    dot_general x8, matrix products, update(): jnp.einsum('rkhd,knd->rkhn', query_heads, kv_piece[:, :, :head_dim], pref...  38.4 us
    reduce_sum x8, other arithmetic, update(): row_sum = row_sum * factor + jnp.sum(expterm, axis=-1)  12.6 us
  transfers between devices with their start and end apart: 2, of which 2 were waited for; matrix products, arithmetic and copies ran while one was open for 0% of the time, Pallas kernels for 0%

commit v1 on v0

--- a/solution.py
+++ b/solution.py
@@ -2,6 +2,7 @@
 import jax.numpy as jnp
 from jax import lax
 from jax.sharding import PartitionSpec as P
+from jax.lax import all_to_all, axis_size
 
 
 def block_count(total_rows, limit_rows):
@@ -81,7 +82,10 @@
         jnp.zeros((text_rows, local_heads, query_count), jnp.float32),
         jnp.zeros((text_rows, local_heads, query_count, head_dim), jnp.float32),
     )
-    gathered = lax.all_gather(kv_block, ("segment", "seq"), axis=1, tiled=True)
+    x_now = axis_size(("segment", "seq"))
+    outcome_arr = jnp.stack([kv_block] * x_now)
+    r2 = all_to_all(outcome_arr, axis_name=("segment", "seq"), split_axis=0, concat_axis=0)
+    gathered = jnp.concatenate(r2, axis=1)
     total_rows = gathered.shape[1]
     blocks = block_count(total_rows, 768)
     block_rows = total_rows // blocks

time: 336 us -> 370 us (1.10)
  waiting for transfers between devices: 215 us -> 231 us
  starting transfers between devices: 0.08 us -> 15.6 us
    all_to_all x0 -> x1, waiting for transfers between devices: none -> 140 us  [shards(): all_to_all(outcome_arr, axis_name=('segment', 'seq'), split_axis=0, conca...]
    all_gather x1 -> x0, waiting for transfers between devices: 124 us -> none  [shards(): gathered = lax.all_gather(kv_block, ('segment', 'seq'), axis=1, tiled=True)]
    all_to_all x0 -> x1, starting transfers between devices: none -> 15.6 us  [shards(): all_to_all(outcome_arr, axis_name=('segment', 'seq'), split_axis=0, conca...]
where the time goes in v1:
time: 370 us; the launch traced here: 369 us
  waiting for transfers between devices  231 us (62%)
  matrix products  83.6 us (23%)
  other arithmetic  19.5 us (5%)
  starting transfers between devices  15.6 us (4%)
  between operations  13.5 us (4%)
  local copies, waits for them, and re-layouts  5.39 us (1%)
    all_to_all x1, waiting for transfers between devices, shards(): all_to_all(outcome_arr, axis_name=('segment', 'seq'), split_axis=0, conca...  140 us
    reduce_scatter x1, waiting for transfers between devices, shards(): lax.psum_scatter(jnp.einsum('rd,dch->crh', vision_states, weight_heads, p...  90.7 us
    dot_general x8, matrix products, update(): jnp.einsum('rkhn,knd->rkhd', weights, kv_piece[:, :, head_dim:], preferre...  41.4 us
    dot_general x8, matrix products, update(): jnp.einsum('rkhd,knd->rkhn', query_heads, kv_piece[:, :, :head_dim], pref...  38.4 us
    all_to_all x1, starting transfers between devices, shards(): all_to_all(outcome_arr, axis_name=('segment', 'seq'), split_axis=0, conca...  15.6 us
    reduce_sum x8, other arithmetic, update(): row_sum = row_sum * factor + jnp.sum(expterm, axis=-1)  12.6 us
  transfers between devices with their start and end apart: 2, of which 2 were waited for; matrix products, arithmetic and copies ran while one was open for 0% of the time, Pallas kernels for 0%

profile of v1, /device:TPU:1, one launch (start us, length us, event | category | flops | bytes accessed | tf_op | source)
XLA Modules:
  0.0 369.4 jit_solution(16309100796999602713)
XLA Ops:
  6.5 0.9 copy-done
  7.5 3.8 %fusion.30 = f32[8,96,256]{2,1,0:T(8,128)} fusion(bf16[120,8,8,256]{3,2,1,0:T(8,128)(2,1)} %bitcast.112, bf16[96,960]{1,0:T(8,128)(2,1)S(1)} %copy-done), kind=kOutput, calls=%fused_computation.41 | convolution fusion | flops 377487360 | bytes 4902912 | tf_op jit(solution)/shard_map/rd,dch->crh/dot_general | solution.py:61
  11.2 90.7 %reduce-scatter.2.cloned.1.call-done = f32[1,96,256]{2,1,0:T(8,128)} async-done(((f32[8,96,256]{2,1,0:T(8,128)}), f32[1,96,256]{2,1,0:T(8,128)}) %reduce-scatter.2.cloned.1.call-update) | async-done | bytes 98320 | tf_op jit(solution)/shard_map/reduce_scatter | solution.py:60
  102.0 0.9 multiply_reduce_fusion
  102.9 0.8 fusion.35
  103.7 0.9 fusion.34
  104.6 2.0 stack.2
  106.6 15.6 %all-to-all-start = ((bf16[64,1,96,256]{3,2,1,0:T(8,128)(2,1)}), bf16[64,1,96,256]{3,2,1,0:T(8,128)(2,1)}, u32[]{:S(2)}, u32[]{:S(2)}) async-start(bf16[64,1,96,256]{3,2,1,0:T(8,128)(2,1)} %stack.2), calls=%async_computation.1 | async-start | bytes 6291456 | tf_op jit(solution)/shard_map/all_to_all | solution.py:87
  122.3 0.2 copy.26
  122.6 0.3 copy.27
  122.9 140.4 %all-to-all-done = bf16[64,1,96,256]{3,2,1,0:T(8,128)(2,1)} async-done(((bf16[64,1,96,256]{3,2,1,0:T(8,128)(2,1)}), bf16[64,1,96,256]{3,2,1,0:T(8,128)(2,1)}, u32[]{:S(2)}, u32[]{:S(2)}) %all-to-all-start) | async-done | bytes 3145760 | tf_op jit(solution)/shard_map/all_to_all | solution.py:87
  263.3 98.1 %while.20 = (s32[]{:T(128)}, f32[512,1,4]{0,2,1:T(4,128)S(1)}, f32[512,1,4]{0,2,1:T(4,128)S(1)}, f32[512,1,4,128]{0,3,2,1:T(8,128)S(1)}, s32[4]{0:T(128)S(1)}, /...) while((s32[]{:T(128)}, f32[512,1,4]{0,2,1:T(4,128)S(1)}, ...), condition=%wide.region_6.7_spmd.clone, body=%wide.region_2.6_spmd.clone.sunk | while | flops 828146688 | bytes 48780040 | solution.py:99
  263.3 0.1 select_reduce_fusion.2
  263.4 0.5 compare_and_fusion.2
  263.9 4.8 %fusion.45 = (f32[512,4]{0,1:T(4,128)S(1)}, f32[768,512,4]{1,0,2:T(8,128)}) fusion(pred[512,768]{0,1:T(8,128)(4,1)S(1)} %compare_and_fusion.2, bf16[512,1,4,128]{3,0,2,1:T(8,128)(2,1)S(1)} %get-tuple-element.411, bf16[1,6144,256]{2,1,0:T(8,128)(2,1)} %get-tuple-element.410, s32[]{:T(128)S(6)} %select_n.147), kind=kOutput, calls=%fused_computation.2.clone.1 | convolution fusion | flops 407369728 | bytes 7413764 | tf_op jit(solution)/shard_map/while/body/eval_jaxpr/rkhd,knd->rkhn/dot_general | solution.py:33
  268.7 5.2 %fusion.48 = f32[512,1,4,128]{0,3,2,1:T(8,128)S(1)} fusion(f32[768,512,4]{1,0,2:T(8,128)} %get-tuple-element.373, f32[512,4]{0,1:T(4,128)S(1)} %bitcast.105, pred[512,768]{0,1:T(8,128)(4,1)S(1)} %compare_and_fusion.2, f32[512,1,4,128]{0,3,2,1:T(8,128)S(1)} %get-tuple-element.392, f32[512,4]{0,1:T(4,128)S(1)} %get-tuple-element.374, ...), kind=kOutput, calls=%fused_computation.10.clone.1 | convolution fusion | flops 411303936 | bytes 8994825 | tf_op jit(solution)/shard_map/while/body/eval_jaxpr/rkhn,knd->rkhd/dot_general | solution.py:48
  273.9 1.6 fusion.47
  275.6 0.1 select_reduce_fusion.2
  275.7 0.5 compare_and_fusion.2
  276.2 4.8 %fusion.45 = (f32[512,4]{0,1:T(4,128)S(1)}, f32[768,512,4]{1,0,2:T(8,128)}) fusion(pred[512,768]{0,1:T(8,128)(4,1)S(1)} %compare_and_fusion.2, bf16[512,1,4,128]{3,0,2,1:T(8,128)(2,1)S(1)} %get-tuple-element.411, bf16[1,6144,256]{2,1,0:T(8,128)(2,1)} %get-tuple-element.410, s32[]{:T(128)S(6)} %select_n.147), kind=kOutput, calls=%fused_computation.2.clone.1 | convolution fusion | flops 407369728 | bytes 7413764 | tf_op jit(solution)/shard_map/while/body/eval_jaxpr/rkhd,knd->rkhn/dot_general | solution.py:33
  281.0 5.2 %fusion.48 = f32[512,1,4,128]{0,3,2,1:T(8,128)S(1)} fusion(f32[768,512,4]{1,0,2:T(8,128)} %get-tuple-element.373, f32[512,4]{0,1:T(4,128)S(1)} %bitcast.105, pred[512,768]{0,1:T(8,128)(4,1)S(1)} %compare_and_fusion.2, f32[512,1,4,128]{0,3,2,1:T(8,128)S(1)} %get-tuple-element.392, f32[512,4]{0,1:T(4,128)S(1)} %get-tuple-element.374, ...), kind=kOutput, calls=%fused_computation.10.clone.1 | convolution fusion | flops 411303936 | bytes 8994825 | tf_op jit(solution)/shard_map/while/body/eval_jaxpr/rkhn,knd->rkhd/dot_general | solution.py:48
  286.2 1.6 fusion.47
  287.9 0.5 compare_and_fusion.2
  288.4 4.8 %fusion.45 = (f32[512,4]{0,1:T(4,128)S(1)}, f32[768,512,4]{1,0,2:T(8,128)}) fusion(pred[512,768]{0,1:T(8,128)(4,1)S(1)} %compare_and_fusion.2, bf16[512,1,4,128]{3,0,2,1:T(8,128)(2,1)S(1)} %get-tuple-element.411, bf16[1,6144,256]{2,1,0:T(8,128)(2,1)} %get-tuple-element.410, s32[]{:T(128)S(6)} %select_n.147), kind=kOutput, calls=%fused_computation.2.clone.1 | convolution fusion | flops 407369728 | bytes 7413764 | tf_op jit(solution)/shard_map/while/body/eval_jaxpr/rkhd,knd->rkhn/dot_general | solution.py:33
  293.3 5.2 %fusion.48 = f32[512,1,4,128]{0,3,2,1:T(8,128)S(1)} fusion(f32[768,512,4]{1,0,2:T(8,128)} %get-tuple-element.373, f32[512,4]{0,1:T(4,128)S(1)} %bitcast.105, pred[512,768]{0,1:T(8,128)(4,1)S(1)} %compare_and_fusion.2, f32[512,1,4,128]{0,3,2,1:T(8,128)S(1)} %get-tuple-element.392, f32[512,4]{0,1:T(4,128)S(1)} %get-tuple-element.374, ...), kind=kOutput, calls=%fused_computation.10.clone.1 | convolution fusion | flops 411303936 | bytes 8994825 | tf_op jit(solution)/shard_map/while/body/eval_jaxpr/rkhn,knd->rkhd/dot_general | solution.py:48
  298.5 1.6 fusion.47
  300.2 0.5 compare_and_fusion.2
  300.7 4.8 %fusion.45 = (f32[512,4]{0,1:T(4,128)S(1)}, f32[768,512,4]{1,0,2:T(8,128)}) fusion(pred[512,768]{0,1:T(8,128)(4,1)S(1)} %compare_and_fusion.2, bf16[512,1,4,128]{3,0,2,1:T(8,128)(2,1)S(1)} %get-tuple-element.411, bf16[1,6144,256]{2,1,0:T(8,128)(2,1)} %get-tuple-element.410, s32[]{:T(128)S(6)} %select_n.147), kind=kOutput, calls=%fused_computation.2.clone.1 | convolution fusion | flops 407369728 | bytes 7413764 | tf_op jit(solution)/shard_map/while/body/eval_jaxpr/rkhd,knd->rkhn/dot_general | solution.py:33
  305.5 5.2 %fusion.48 = f32[512,1,4,128]{0,3,2,1:T(8,128)S(1)} fusion(f32[768,512,4]{1,0,2:T(8,128)} %get-tuple-element.373, f32[512,4]{0,1:T(4,128)S(1)} %bitcast.105, pred[512,768]{0,1:T(8,128)(4,1)S(1)} %compare_and_fusion.2, f32[512,1,4,128]{0,3,2,1:T(8,128)S(1)} %get-tuple-element.392, f32[512,4]{0,1:T(4,128)S(1)} %get-tuple-element.374, ...), kind=kOutput, calls=%fused_computation.10.clone.1 | convolution fusion | flops 411303936 | bytes 8994825 | tf_op jit(solution)/shard_map/while/body/eval_jaxpr/rkhn,knd->rkhd/dot_general | solution.py:48
  310.7 1.6 fusion.47
  312.5 0.5 compare_and_fusion.2
  313.0 4.8 %fusion.45 = (f32[512,4]{0,1:T(4,128)S(1)}, f32[768,512,4]{1,0,2:T(8,128)}) fusion(pred[512,768]{0,1:T(8,128)(4,1)S(1)} %compare_and_fusion.2, bf16[512,1,4,128]{3,0,2,1:T(8,128)(2,1)S(1)} %get-tuple-element.411, bf16[1,6144,256]{2,1,0:T(8,128)(2,1)} %get-tuple-element.410, s32[]{:T(128)S(6)} %select_n.147), kind=kOutput, calls=%fused_computation.2.clone.1 | convolution fusion | flops 407369728 | bytes 7413764 | tf_op jit(solution)/shard_map/while/body/eval_jaxpr/rkhd,knd->rkhn/dot_general | solution.py:33
  317.8 5.2 %fusion.48 = f32[512,1,4,128]{0,3,2,1:T(8,128)S(1)} fusion(f32[768,512,4]{1,0,2:T(8,128)} %get-tuple-element.373, f32[512,4]{0,1:T(4,128)S(1)} %bitcast.105, pred[512,768]{0,1:T(8,128)(4,1)S(1)} %compare_and_fusion.2, f32[512,1,4,128]{0,3,2,1:T(8,128)S(1)} %get-tuple-element.392, f32[512,4]{0,1:T(4,128)S(1)} %get-tuple-element.374, ...), kind=kOutput, calls=%fused_computation.10.clone.1 | convolution fusion | flops 411303936 | bytes 8994825 | tf_op jit(solution)/shard_map/while/body/eval_jaxpr/rkhn,knd->rkhd/dot_general | solution.py:48
  323.0 1.6 fusion.47
  324.7 0.5 compare_and_fusion.2
  325.2 4.8 %fusion.45 = (f32[512,4]{0,1:T(4,128)S(1)}, f32[768,512,4]{1,0,2:T(8,128)}) fusion(pred[512,768]{0,1:T(8,128)(4,1)S(1)} %compare_and_fusion.2, bf16[512,1,4,128]{3,0,2,1:T(8,128)(2,1)S(1)} %get-tuple-element.411, bf16[1,6144,256]{2,1,0:T(8,128)(2,1)} %get-tuple-element.410, s32[]{:T(128)S(6)} %select_n.147), kind=kOutput, calls=%fused_computation.2.clone.1 | convolution fusion | flops 407369728 | bytes 7413764 | tf_op jit(solution)/shard_map/while/body/eval_jaxpr/rkhd,knd->rkhn/dot_general | solution.py:33
  330.1 5.2 %fusion.48 = f32[512,1,4,128]{0,3,2,1:T(8,128)S(1)} fusion(f32[768,512,4]{1,0,2:T(8,128)} %get-tuple-element.373, f32[512,4]{0,1:T(4,128)S(1)} %bitcast.105, pred[512,768]{0,1:T(8,128)(4,1)S(1)} %compare_and_fusion.2, f32[512,1,4,128]{0,3,2,1:T(8,128)S(1)} %get-tuple-element.392, f32[512,4]{0,1:T(4,128)S(1)} %get-tuple-element.374, ...), kind=kOutput, calls=%fused_computation.10.clone.1 | convolution fusion | flops 411303936 | bytes 8994825 | tf_op jit(solution)/shard_map/while/body/eval_jaxpr/rkhn,knd->rkhd/dot_general | solution.py:48
  335.2 1.6 fusion.47
  337.0 0.5 compare_and_fusion.2
  337.5 4.8 %fusion.45 = (f32[512,4]{0,1:T(4,128)S(1)}, f32[768,512,4]{1,0,2:T(8,128)}) fusion(pred[512,768]{0,1:T(8,128)(4,1)S(1)} %compare_and_fusion.2, bf16[512,1,4,128]{3,0,2,1:T(8,128)(2,1)S(1)} %get-tuple-element.411, bf16[1,6144,256]{2,1,0:T(8,128)(2,1)} %get-tuple-element.410, s32[]{:T(128)S(6)} %select_n.147), kind=kOutput, calls=%fused_computation.2.clone.1 | convolution fusion | flops 407369728 | bytes 7413764 | tf_op jit(solution)/shard_map/while/body/eval_jaxpr/rkhd,knd->rkhn/dot_general | solution.py:33
  342.3 5.2 %fusion.48 = f32[512,1,4,128]{0,3,2,1:T(8,128)S(1)} fusion(f32[768,512,4]{1,0,2:T(8,128)} %get-tuple-element.373, f32[512,4]{0,1:T(4,128)S(1)} %bitcast.105, pred[512,768]{0,1:T(8,128)(4,1)S(1)} %compare_and_fusion.2, f32[512,1,4,128]{0,3,2,1:T(8,128)S(1)} %get-tuple-element.392, f32[512,4]{0,1:T(4,128)S(1)} %get-tuple-element.374, ...), kind=kOutput, calls=%fused_computation.10.clone.1 | convolution fusion | flops 411303936 | bytes 8994825 | tf_op jit(solution)/shard_map/while/body/eval_jaxpr/rkhn,knd->rkhd/dot_general | solution.py:48
  347.5 1.6 fusion.47
  349.3 0.5 compare_and_fusion.2
  349.7 4.8 %fusion.45 = (f32[512,4]{0,1:T(4,128)S(1)}, f32[768,512,4]{1,0,2:T(8,128)}) fusion(pred[512,768]{0,1:T(8,128)(4,1)S(1)} %compare_and_fusion.2, bf16[512,1,4,128]{3,0,2,1:T(8,128)(2,1)S(1)} %get-tuple-element.411, bf16[1,6144,256]{2,1,0:T(8,128)(2,1)} %get-tuple-element.410, s32[]{:T(128)S(6)} %select_n.147), kind=kOutput, calls=%fused_computation.2.clone.1 | convolution fusion | flops 407369728 | bytes 7413764 | tf_op jit(solution)/shard_map/while/body/eval_jaxpr/rkhd,knd->rkhn/dot_general | solution.py:33
  354.6 5.2 %fusion.48 = f32[512,1,4,128]{0,3,2,1:T(8,128)S(1)} fusion(f32[768,512,4]{1,0,2:T(8,128)} %get-tuple-element.373, f32[512,4]{0,1:T(4,128)S(1)} %bitcast.105, pred[512,768]{0,1:T(8,128)(4,1)S(1)} %compare_and_fusion.2, f32[512,1,4,128]{0,3,2,1:T(8,128)S(1)} %get-tuple-element.392, f32[512,4]{0,1:T(4,128)S(1)} %get-tuple-element.374, ...), kind=kOutput, calls=%fused_computation.10.clone.1 | convolution fusion | flops 411303936 | bytes 8994825 | tf_op jit(solution)/shard_map/while/body/eval_jaxpr/rkhn,knd->rkhd/dot_general | solution.py:48
  359.8 1.6 fusion.47
  361.4 0.1 divide_convert_fusion
  361.5 1.0 copy.31
  (79 shorter events, 1.1 us)
Async XLA Ops:
  6.5 0.9 copy-start
  6.5 95.4 %reduce-scatter.2.cloned.1.call-start = ((), (), s32[]{:S(2)}) async-start(), calls=%async_computation.2 | async-start | bytes 884736 | tf_op jit(solution)/shard_map/reduce_scatter | solution.py:60
  11.2 111.1 %copy-start.2 = (bf16[512,1,512]{2,0,1:T(8,128)(2,1)S(1)}, bf16[512,1,512]{2,0,1:T(8,128)(2,1)}, u32[]{:S(2)}) copy-start(bf16[512,1,512]{2,0,1:T(8,128)(2,1)} %param.11) | copy-start | bytes 1572868
  11.2 111.7 %copy-start.3 = (s32[512,2]{0,1:T(2,128)S(1)}, s32[512,2]{0,1:T(2,128)}, u32[]{:S(2)}) copy-start(s32[512,2]{0,1:T(2,128)} %param.13) | copy-start | bytes 12292
  11.2 252.1 %copy-start.4 = (s32[4]{0:T(128)S(1)}, s32[4]{0:T(128)}, u32[]{:S(2)}) copy-start(s32[4]{0:T(128)} %param.12) | copy-start | bytes 52
  106.6 156.7 %all-to-all-start = ((bf16[64,1,96,256]{3,2,1,0:T(8,128)(2,1)}), bf16[64,1,96,256]{3,2,1,0:T(8,128)(2,1)}, u32[]{:S(2)}, u32[]{:S(2)}) async-start(bf16[64,1,96,256]{3,2,1,0:T(8,128)(2,1)} %stack.2), calls=%async_computation.1 | async-start | bytes 6291456 | tf_op jit(solution)/shard_map/all_to_all | solution.py:87
  268.7 5.2 %copy-start.1 = (f32[768,512,4]{1,0,2:T(8,128)S(1)}, f32[768,512,4]{1,0,2:T(8,128)}, u32[]{:S(2)}) copy-start(f32[768,512,4]{1,0,2:T(8,128)} %get-tuple-element.373) | copy-start | bytes 18874372 | tf_op jit(solution)/shard_map/while
  281.0 5.2 %copy-start.1 = (f32[768,512,4]{1,0,2:T(8,128)S(1)}, f32[768,512,4]{1,0,2:T(8,128)}, u32[]{:S(2)}) copy-start(f32[768,512,4]{1,0,2:T(8,128)} %get-tuple-element.373) | copy-start | bytes 18874372 | tf_op jit(solution)/shard_map/while
  293.3 5.2 %copy-start.1 = (f32[768,512,4]{1,0,2:T(8,128)S(1)}, f32[768,512,4]{1,0,2:T(8,128)}, u32[]{:S(2)}) copy-start(f32[768,512,4]{1,0,2:T(8,128)} %get-tuple-element.373) | copy-start | bytes 18874372 | tf_op jit(solution)/shard_map/while
  305.5 5.2 %copy-start.1 = (f32[768,512,4]{1,0,2:T(8,128)S(1)}, f32[768,512,4]{1,0,2:T(8,128)}, u32[]{:S(2)}) copy-start(f32[768,512,4]{1,0,2:T(8,128)} %get-tuple-element.373) | copy-start | bytes 18874372 | tf_op jit(solution)/shard_map/while
  317.8 5.2 %copy-start.1 = (f32[768,512,4]{1,0,2:T(8,128)S(1)}, f32[768,512,4]{1,0,2:T(8,128)}, u32[]{:S(2)}) copy-start(f32[768,512,4]{1,0,2:T(8,128)} %get-tuple-element.373) | copy-start | bytes 18874372 | tf_op jit(solution)/shard_map/while
  330.0 5.2 %copy-start.1 = (f32[768,512,4]{1,0,2:T(8,128)S(1)}, f32[768,512,4]{1,0,2:T(8,128)}, u32[]{:S(2)}) copy-start(f32[768,512,4]{1,0,2:T(8,128)} %get-tuple-element.373) | copy-start | bytes 18874372 | tf_op jit(solution)/shard_map/while
  342.3 5.2 %copy-start.1 = (f32[768,512,4]{1,0,2:T(8,128)S(1)}, f32[768,512,4]{1,0,2:T(8,128)}, u32[]{:S(2)}) copy-start(f32[768,512,4]{1,0,2:T(8,128)} %get-tuple-element.373) | copy-start | bytes 18874372 | tf_op jit(solution)/shard_map/while
  354.6 5.2 %copy-start.1 = (f32[768,512,4]{1,0,2:T(8,128)S(1)}, f32[768,512,4]{1,0,2:T(8,128)}, u32[]{:S(2)}) copy-start(f32[768,512,4]{1,0,2:T(8,128)} %get-tuple-element.373) | copy-start | bytes 18874372 | tf_op jit(solution)/shard_map/while
Sparse Core Ops, SparseCore 0:
  11.8 90.1 reduce-scatter.1
